TPU v7x, 128 devices: a whole 4x4x4 slice. The times are simulated.
128 devices in a mesh: req: 16 (over z, y), mlp: 8 (over x, core).
Axes of the slice: x: 4, y: 4, z: 4, core: 2. Of those that a mesh axis runs over, the one named last changes fastest.
Arguments:
- prompt_rows: bfloat16 [32768, 1792], P(('req', 'mlp')), may hold values from -6 to 6
- prompt_edge: bfloat16 [128, 2, 1792], P(('req', 'mlp')), may hold values from -6 to 6
- decode_rows: bfloat16 [512, 1792], P(('req', 'mlp')), may hold values from -6 to 6
- decode_edge: bfloat16 [512, 2, 1792], P(('req', 'mlp')), may hold values from -6 to 6
- decode_live: int32 [512], P(('req', 'mlp')), may hold values 0 or 1
- cache_length: int32 [512], P(('req', 'mlp')), may hold values from 1 to 32768, as said below
- cache_state: float32 [512, 273, 1792], P(('req', 'mlp')), as said below
- cache_keysum: float32 [512, 272, 16], P(('req', 'mlp')), as said below
- prefix_length: int32 [8], P('mlp'), may hold values from 256 to 2048, as said below
- prefix_state: float32 [8, 273, 1792], P('mlp', None, 'req'), as said below
- prefix_keysum: float32 [8, 272, 16], P('mlp', None, 'req'), as said below
- conv_gain: float32 [1792], replicated, may hold values from 0.5 to 1.5
- conv_taps: float32 [3, 1792], replicated, may hold values from -3 to 3
- attend_gain: float32 [1792], replicated, may hold values from 0.5 to 1.5
- feature_weight: bfloat16 [1792, 512], replicated, may hold values from -0.125 to 0.125
- value_weight: bfloat16 [1792, 1792], replicated, may hold values from -0.125 to 0.125
- output_weight: bfloat16 [1792, 1792], replicated, may hold values from -0.125 to 0.125
- hidden_gain: float32 [1792], replicated, may hold values from 0.5 to 1.5
- gate_up: bfloat16 [2, 1792, 3584], P(None, 'req', 'mlp'), may hold values from -0.125 to 0.125
- down_weight: bfloat16 [3584, 1792], P('mlp', 'req'), may hold values from -0.09375 to 0.09375
Outputs:
- prompt_out: bfloat16 [32768, 1792], P(('req', 'mlp'))
- decode_out: bfloat16 [512, 1792], P(('req', 'mlp'))
Inputs may be any that keep to these rules, and one draw needn't show every extreme that they name: `cache_length`: every slot's length is at least 1; some slot holds exactly 32768 tokens. `cache_state`: drawn as cache_length times the mean of phi(k) v^T over a few sampled keys k and values v of each head, plus independent noise of size sqrt(cache_length). `cache_keysum`: drawn as cache_length times the mean of phi_rest over the same sampled keys, so that cache_length + phi_rest(q) . cache_keysum is a sum of positive terms. `prefix_length`: A multiple of 256; some group's prefix is exactly 2048 tokens. `prefix_state`: drawn as prefix_length times the mean of phi(k) v^T over a few sampled keys and values of each head, plus independent noise of size sqrt(prefix_length). `prefix_keysum`: prefix_length times the mean of phi_rest over the same sampled keys.
All inputs are finite; a program needn't handle non-finite values. No bound on the sum of `decode_live` on one device may be relied on, other than what follows from the above.
Results may differ from a plain program's by a relative error of at most 0.014.
Values may be sent and summed in bfloat16 or wider, within the bound.
A program may use at most 128 MiB of HBM per device.

v0:
```python
import jax
import jax.numpy as jnp
from jax import lax
from jax.experimental import pallas as pl
from jax.experimental.pallas import tpu as pltpu
from jax.sharding import Mesh
from jax.sharding import PartitionSpec as P

D = 1792
H = 16
FD = 16
DV = 112
NF = 273
T = 256
R = 272
MESH = pl.DeviceIdType.MESH

F32 = jnp.float32
BF = jnp.bfloat16
epsilon = 1e-06

ORDERS = (("y", "z", "x"), ("z", "x", "y"), ("x", "y", "z"), ("y", "z"))
GATE, DOWN, UP, PREFIX = range(4)


def dot(a, b):
    return jnp.dot(a, b, preferred_element_type=F32)


def dot_t(a, b):
    return lax.dot_general(a, b, (((1,), (1,)), ((), ())), preferred_element_type=F32)


def norm(values, gain):
    return values * lax.rsqrt(jnp.mean(values * values, axis=-1, keepdims=True) + epsilon) * gain


def iota(shape, dim):
    return lax.broadcasted_iota(jnp.int32, shape, dim)


def layer_kernel(
    rows_ref, edge_ref, slots_ref, slot_two_ref, slot_one_ref, keysum_ref,
    conv_gain_ref, taps_ref, attend_gain_ref, hidden_gain_ref,
    gate_in, down_in, up_in, prefix_in, cache_in, wf_in, wv_in, wo_in,
    out_ref,
    gate, down, up, prefix, wf, wv, wo, cache,
    big, conv, ain, qk, rep, slot_att, pair, tok, attended, hid, give, take, fin,
    local_sem, cache_sem, send_sem, recv_sem, swap_send, swap_recv,
):
    my = {a: lax.axis_index(a) for a in ("z", "y", "x")}
    core = lax.axis_index("c")
    other = 1 - core

    def near(axis, step):
        return lax.rem(my[axis] + (4 + step), 4)

    local = []
    for k, (source, target) in enumerate(((wf_in, wf), (wv_in, wv), (wo_in, wo.at[pl.ds(0, D)]))):
        copy = pltpu.make_async_copy(source, target, local_sem.at[4 + k])
        copy.start()
        local.append(copy)
    cache_copies = []
    for n in range(4):
        cache_copies.append(pltpu.make_async_copy(cache_in.at[n], cache.at[n % 2], cache_sem.at[n]))
    cache_copies[0].start()
    cache_copies[1].start()

    def view(part, sel):
        if part == DOWN:
            z, y = sel["z"], sel["y"]
            if isinstance(z, tuple):
                lanes = pl.ds(pl.multiple_of(y * 512 + z[0] * 128, 128), z[1] * 128)
            else:
                lanes = pl.ds(pl.multiple_of(y * 512 + z * 128, 128), 128)
            x = sel["x"]
            return down.at[pl.ds(*x) if isinstance(x, tuple) else x, :, lanes]
        index = [pl.ds(*sel[a]) if isinstance(sel[a], tuple) else sel[a] for a in ("x", "z", "y")]
        if part == PREFIX:
            return prefix.at[index[1], index[2]]
        return (gate, None, up)[part].at[index[0], index[1], index[2]]

    barrier = pltpu.get_barrier_semaphore()
    for axis in ("z", "y", "x"):
        for step in (1, -1):
            pl.semaphore_signal(barrier, inc=1, device_id={axis: near(axis, step)}, device_id_type=MESH)
    pl.semaphore_signal(barrier, inc=1, device_id={"c": other}, device_id_type=MESH)
    own = []
    for part, source in ((PREFIX, prefix_in), (GATE, gate_in), (DOWN, down_in), (UP, up_in)):
        copy = pltpu.make_async_copy(source, view(part, my), local_sem.at[part])
        copy.start()
        own.append(copy)
    pl.semaphore_wait(barrier, 7)
    for copy in own:
        copy.wait()

    started = []

    def send(part, sel, axis, step, k):
        block = view(part, sel)
        copy = pltpu.make_async_remote_copy(
            block, block, send_sem.at[part, k], recv_sem.at[part, k],
            device_id={axis: near(axis, step)}, device_id_type=MESH)
        copy.start()
        started.append(copy)

    def arrived(part, sel, k):
        block = view(part, sel)
        pltpu.make_async_remote_copy(
            block, block, send_sem.at[part, k], recv_sem.at[part, k],
            device_id={"x": near("x", 1)}, device_id_type=MESH).wait_recv()

    FULL, LOW, HIGH = (0, 4), (0, 2), (2, 2)

    def phase_one(part):
        axis = ORDERS[part][0]
        send(part, my, axis, 1, 0)
        send(part, my, axis, -1, 1)

    def phase_one_on(part):
        axis = ORDERS[part][0]
        sel = {**my, axis: near(axis, -1)}
        arrived(part, sel, 0)
        send(part, sel, axis, 1, 2)

    def phase_one_end(part):
        axis = ORDERS[part][0]
        arrived(part, {**my, axis: near(axis, 1)}, 1)
        arrived(part, {**my, axis: near(axis, 2)}, 2)

    def phase(part, number):
        first, axis = ORDERS[part][0], ORDERS[part][number]
        held = {**my, **{a: FULL for a in ORDERS[part][:number]}}
        k = 3 + 6 * (number - 1)
        send(part, {**held, first: LOW}, axis, 1, k)
        send(part, {**held, first: HIGH}, axis, -1, k + 1)
        send(part, {**held, first: HIGH}, axis, 1, k + 2)
        send(part, {**held, first: LOW}, axis, -1, k + 3)

    def phase_on(part, number):
        first, axis = ORDERS[part][0], ORDERS[part][number]
        held = {**my, **{a: FULL for a in ORDERS[part][:number]}}
        k = 3 + 6 * (number - 1)
        sel = {**held, first: LOW, axis: near(axis, -1)}
        arrived(part, sel, k)
        send(part, sel, axis, 1, k + 4)
        sel = {**held, first: HIGH, axis: near(axis, 1)}
        arrived(part, sel, k + 1)
        send(part, sel, axis, -1, k + 5)

    def phase_near(part, number):
        first, axis = ORDERS[part][0], ORDERS[part][number]
        held = {**my, **{a: FULL for a in ORDERS[part][:number]}}
        k = 3 + 6 * (number - 1)
        arrived(part, {**held, first: HIGH, axis: near(axis, -1)}, k + 2)
        arrived(part, {**held, first: LOW, axis: near(axis, 1)}, k + 3)

    def phase_far(part, number):
        first, axis = ORDERS[part][0], ORDERS[part][number]
        held = {**my, **{a: FULL for a in ORDERS[part][:number]}}
        k = 3 + 6 * (number - 1)
        arrived(part, {**held, first: LOW, axis: near(axis, 2)}, k + 4)
        arrived(part, {**held, first: HIGH, axis: near(axis, 2)}, k + 5)

    everything = (PREFIX, GATE, DOWN, UP)
    for part in everything:
        phase_one(part)

    conv_gain = conv_gain_ref[...]
    big[0:8, 0:D] = edge_ref[...]

    def norm_rows(i, _):
        at = pl.multiple_of(i * 16, 16)
        u = norm(rows_ref[pl.ds(at, 16), :].astype(F32), conv_gain)
        big[pl.ds(pl.multiple_of(at + 8, 8), 16), 0:D] = u.astype(BF).astype(F32)
        return 0

    lax.fori_loop(0, T // 16, norm_rows, 0)
    for part in everything:
        phase_one_on(part)

    def gated(rows, u, one, two):
        convolved = taps_ref[0:1, :] * u + taps_ref[1:2, :] * one + taps_ref[2:3, :] * two
        mixed = (rows.astype(F32) + convolved * jax.nn.sigmoid(u)).astype(BF)
        return mixed, norm(mixed.astype(F32), attend_gain_ref[...]).astype(BF)

    def conv_rows(i, _):
        at = pl.multiple_of(i * 16, 16)
        window = big[pl.ds(at, 24), 0:D]
        mixed, normed = gated(
            rows_ref[pl.ds(at, 16), :], window[8:], pltpu.roll(window, 1, 0)[8:], pltpu.roll(window, 2, 0)[8:])
        conv[pl.ds(at, 16), :] = mixed
        ain[pl.ds(at, 16), :] = normed
        return 0

    lax.fori_loop(0, T // 16, conv_rows, 0)
    slot_u = norm(slots_ref[...].astype(F32), conv_gain).astype(BF).astype(F32)
    mixed, normed = gated(slots_ref[...], slot_u, slot_one_ref[...].astype(F32), slot_two_ref[...].astype(F32))
    conv[T:R, :] = mixed
    ain[T:R, :] = normed

    for part in everything:
        phase_one_end(part)
        phase(part, 1)

    local[0].wait()
    qk[...] = dot(ain[...], wf[...]).astype(BF)
    local[1].wait()

    def value_columns(j, _):
        at = pl.multiple_of(j * 256, 256)
        big[0:R, pl.ds(at, 256)] = dot(ain[...], wv[:, pl.ds(at, 256)]).astype(BF).astype(F32)
        return 0

    lax.fori_loop(0, 3, value_columns, 0)
    for part in everything:
        phase_on(part, 1)
    lax.fori_loop(3, 7, value_columns, 0)

    lane = iota((256, 256), 1)
    feature = iota((256, 256), 0) & 15
    rep[:, 0:256] = (feature == lane >> 4).astype(F32).astype(BF)
    rep[:, 256:512] = (feature == (lane & 15)).astype(F32).astype(BF)

    wide = iota((256, 384), 1)
    deep = iota((256, 384), 0) & 15
    first_sel = jnp.where(wide < 17, wide - 1, (wide - 17) >> 4)
    first_sel = ((deep == first_sel) & (wide < NF)).astype(F32).astype(BF)
    second_sel = ((deep == ((wide - 17) & 15)) & (wide >= 17) & (wide < NF)).astype(F32).astype(BF)
    column = iota((16, 384), 1)
    first_add = (column == 0).astype(F32)
    second_add = jnp.where(column == 0, 1.0, jnp.where(column < 17, FD ** (-0.25), 0.0))
    head_of = (iota((16, 256), 1) >> 4) == iota((16, 256), 0)
    head_start = iota((16, D), 0) * DV
    value_col = iota((16, D), 1)
    head_cols = (value_col >= head_start) & (value_col < head_start + DV)
    slot_qk = qk[T:R, :].astype(F32)
    slot_v = big[T:R, 0:D]
    slot_att[...] = jnp.zeros_like(slot_att)
    for n in range(4):
        cache_copies[n].wait()
        q = jnp.where(head_of, slot_qk[n:n + 1, 0:256], 0.0)
        s = jnp.sum(q * slot_qk[n:n + 1, 256:512], axis=-1, keepdims=True) * FD ** (-0.5)
        weight = 1.0 + s + 0.5 * s * s
        qb = q.astype(BF)
        phi = (dot(qb, first_sel) + first_add) * (dot(qb, second_sel) * (2.0 * FD) ** (-0.5) + second_add)
        den = jnp.sum(phi * keysum_ref[n], axis=-1, keepdims=True) + weight
        phi_high = phi.astype(BF)
        num = dot(phi_high[:, 0:NF], cache[n % 2].astype(BF))
        if n + 2 < 4:
            cache_copies[n + 2].start()
        heads = (num + weight * slot_v[n:n + 1, :]) / den
        slot_att[n:n + 1, 0:D] = jnp.sum(jnp.where(head_cols, heads, 0.0), axis=0, keepdims=True)

    for part in everything:
        phase_near(part, 1)
        phase_far(part, 1)
        if part != PREFIX:
            phase(part, 2)

    for z in range(4):
        for y in range(4):
            h = z * 4 + y
            rep[h * 16:h * 16 + 16, 512:640] = prefix[z, y, 256:272, :]
    big[R:2 * R, 0:D] = jnp.zeros((R, D), F32)
    local[2].wait()
    wo[D:D + 32, :] = jnp.zeros((32, D), BF)
    causal = iota((T, T), 1) <= iota((T, T), 0)
    lane_head = iota((T, 256), 1) >> 4
    lane128 = iota((T, 128), 1)

    def one_head(h):
        qm = jnp.where(lane_head == h, qk[0:T, 0:256].astype(F32), 0.0).astype(BF)
        s = dot_t(qm, qk[0:T, 256:512]) * FD ** (-0.5)
        w = jnp.where(causal, 1.0 + s + 0.5 * s * s, 0.0).astype(BF)
        start = (h * DV // 128) * 128
        window = big[0:T, pl.ds(pl.multiple_of(start, 128), 256)]
        v = pltpu.roll(window, lax.rem(256 + start - h * DV, 256), 1)[:, 0:128]
        v = jnp.where(lane128 < DV, v, jnp.where(lane128 == DV, 1.0, 0.0)).astype(BF)
        phi = (dot(qm, rep[:, 0:256]) * dot(qm, rep[:, 256:512])).astype(BF)
        state = prefix[h // 4, lax.rem(h, 4)]
        num = dot(w, v) + dot(phi, state[0:256]) + dot(qm, rep[:, 512:640]) + state[272:273].astype(F32)
        return jnp.where(lane128 < DV, num / num[:, DV:DV + 1], 0.0)

    lane256 = iota((T, 256), 1)

    def head_pair(p, _):
        left = one_head(2 * p)
        right = one_head(2 * p + 1)
        both = jnp.concatenate([left, jnp.zeros_like(left)], axis=1)
        both = both + pltpu.roll(jnp.concatenate([right, jnp.zeros_like(right)], axis=1), DV, 1)
        pair[0:T, :] = both.astype(BF)
        start = (p * 224 // 128) * 128
        slots = pltpu.roll(slot_att[:, pl.ds(pl.multiple_of(start, 128), 384)], lax.rem(384 + start - p * 224, 384), 1)
        pair[T:R, :] = jnp.where(lane256[0:16] < 224, slots[:, 0:256], 0.0).astype(BF)
        at = pl.multiple_of(p * 224, 32)
        big[R:2 * R, 0:D] += dot(pair[...], wo[pl.ds(at, 256), :])
        return 0

    lax.fori_loop(0, 4, head_pair, 0)
    lax.fori_loop(4, 8, head_pair, 0)

    def hidden_rows(i, _):
        at = pl.multiple_of(i * 16, 16)
        mixed = (conv[pl.ds(at, 16), :].astype(F32) + big[pl.ds(pl.multiple_of(R + at, 16), 16), 0:D]).astype(BF)
        attended[pl.ds(at, 16), :] = mixed
        tok[core, pl.ds(at, 16), :] = norm(mixed.astype(F32), hidden_gain_ref[...]).astype(BF)
        return 0

    lax.fori_loop(0, R // 16, hidden_rows, 0)
    swap = pltpu.make_async_remote_copy(
        tok.at[core], tok.at[core], swap_send.at[0], swap_recv.at[0], device_id={"c": other}, device_id_type=MESH)
    swap.start()
    for part in (GATE, DOWN, UP):
        phase_on(part, 2)
    swap.wait_send()
    pltpu.make_async_remote_copy(
        tok.at[other], tok.at[other], swap_send.at[0], swap_recv.at[0],
        device_id={"c": other}, device_id_type=MESH).wait_recv()
    for part in (GATE, DOWN, UP):
        phase_near(part, 2)
        phase_far(part, 2)

    lane_half = iota((2 * R, 128), 1)

    def feed(x, _):
        tokens = tok[...].reshape(2 * R, D)
        first = dot(tokens, gate[x].reshape(D, 512))
        second = dot(tokens, up[x].reshape(D, 384))
        hid[x, :, 0:384] = (jax.nn.silu(first[:, 0:384]) * second).astype(BF)
        last = first[:, 384:512]
        last = jax.nn.silu(last) * pltpu.roll(last, 64, 1)
        hid[x, :, 384:512] = jnp.where(lane_half < 64, last, 0.0).astype(BF)
        return 0

    lax.fori_loop(0, 4, feed, 0)

    def contract(j, _):
        lanes = pl.ds(pl.multiple_of(j * 256, 256), 256)
        total = dot(hid[0, :, 0:448], down[0, :, lanes])
        for x in range(1, 4):
            total += dot(hid[x, :, 0:448], down[x, :, lanes])
        big[:, lanes] = total
        return 0

    lax.fori_loop(0, 8, contract, 0)

    give[...] = big[pl.ds(pl.multiple_of(other * R, 16), R), :].astype(BF)
    swap = pltpu.make_async_remote_copy(
        give, take, swap_send.at[1], swap_recv.at[1], device_id={"c": other}, device_id_type=MESH)
    swap.start()
    fin[:, 0:D] = attended[...].astype(F32)
    fin[:, D:D + 128] = jnp.zeros((R, 128), F32)
    swap.wait()
    mine = pl.multiple_of(core * R, 16)
    for r in range(H):
        lanes = ((r % 4) * 4 + r // 4) * 128
        piece = big[pl.ds(mine, R), lanes:lanes + 128] + take[:, lanes:lanes + 128].astype(F32)
        start = r * DV // 128 * 128
        piece = pltpu.roll(jnp.concatenate([piece, jnp.zeros_like(piece)], axis=1), r * DV - start, 1)
        fin[:, start:start + 256] += piece
    out_ref[...] = fin[:, 0:D].astype(BF)
    for copy in started:
        copy.wait_send()


def on_device(
    prompt_rows, prompt_edge, decode_rows, decode_edge, decode_live, cache_length, cache_state,
    cache_keysum, prefix_length, prefix_state, prefix_keysum, conv_gain, conv_taps, attend_gain,
    feature_weight, value_weight, output_weight, hidden_gain, gate_up, down_weight,
):
    gate_in = jnp.concatenate([gate_up[0], gate_up[1, :, 384:]], axis=1)
    up_in = gate_up[1, :, :384]
    down_in = jnp.pad(down_weight, ((0, 0), (0, 16)))
    sums = jnp.concatenate([prefix_length.astype(F32)[:, None], prefix_keysum[0]], axis=0)
    state = jnp.concatenate([prefix_state[0], sums, jnp.zeros((NF, 15), F32)], axis=1)
    prefix_in = jnp.concatenate([
        state[17:] * (2.0 * FD) ** (-0.5), state[1:17] * FD ** (-0.25), state[0:1], jnp.zeros((15, 128), F32)],
        axis=0).astype(BF)
    lengths = jnp.broadcast_to(cache_length.astype(F32)[:, None, None], (4, H, 1))
    keysum = jnp.concatenate(
        [lengths, jnp.transpose(cache_keysum, (0, 2, 1)), jnp.zeros((4, H, 384 - NF), F32)], axis=2)
    edge = jnp.pad(prompt_edge[0].astype(F32), ((6, 0), (0, 0)))
    spare = ((0, 12), (0, 0))
    vmem = pl.BlockSpec(memory_space=pltpu.VMEM)
    hbm = pl.BlockSpec(memory_space=pl.ANY)
    out = pl.pallas_call(
        layer_kernel,
        out_shape=jax.ShapeDtypeStruct((R, D), BF),
        in_specs=[vmem] * 10 + [hbm] * 8,
        out_specs=vmem,
        scratch_shapes=[
            pltpu.VMEM((4, 4, 4, 112, 512), BF),
            pltpu.VMEM((4, 448, 2048), BF),
            pltpu.VMEM((4, 4, 4, 112, 384), BF),
            pltpu.VMEM((4, 4, 288, 128), BF),
            pltpu.VMEM((D, 512), BF),
            pltpu.VMEM((D, D), BF),
            pltpu.VMEM((D + 32, D), BF),
            pltpu.VMEM((2, NF, D), F32),
            pltpu.VMEM((2 * R, 2048), F32),
            pltpu.VMEM((R, D), BF),
            pltpu.VMEM((R, D), BF),
            pltpu.VMEM((R, 512), BF),
            pltpu.VMEM((256, 640), BF),
            pltpu.VMEM((16, 2048), F32),
            pltpu.VMEM((R, 256), BF),
            pltpu.VMEM((2, R, D), BF),
            pltpu.VMEM((R, D), BF),
            pltpu.VMEM((4, 2 * R, 512), BF),
            pltpu.VMEM((R, 2048), BF),
            pltpu.VMEM((R, 2048), BF),
            pltpu.VMEM((R, D + 128), F32),
            pltpu.SemaphoreType.DMA((7,)),
            pltpu.SemaphoreType.DMA((4,)),
            pltpu.SemaphoreType.DMA((4, 15)),
            pltpu.SemaphoreType.DMA((4, 15)),
            pltpu.SemaphoreType.DMA((2,)),
            pltpu.SemaphoreType.DMA((2,)),
        ],
        compiler_params=pltpu.CompilerParams(
            collective_id=0, has_side_effects=True, vmem_limit_bytes=67043328),
    )(
        prompt_rows, edge, jnp.pad(decode_rows, spare), jnp.pad(decode_edge[:, 0], spare),
        jnp.pad(decode_edge[:, 1], spare), keysum, conv_gain[None], conv_taps, attend_gain[None],
        hidden_gain[None], gate_in, down_in, up_in, prefix_in, cache_state, feature_weight,
        value_weight, output_weight,
    )
    slots = out[T:T + 4]
    return out[:T], jnp.where(decode_live[:, None] == 1, slots, jnp.zeros_like(slots))


def solution(mesh):
    torus = Mesh(mesh.devices.reshape(4, 4, 4, 2), ("z", "y", "x", "c"))
    rows, req, mlp = ("z", "y", "x", "c"), ("z", "y"), ("x", "c")
    return jax.shard_map(
        on_device,
        mesh=torus,
        in_specs=(
            P(rows, None), P(rows, None, None), P(rows, None), P(rows, None, None), P(rows), P(rows),
            P(rows, None, None), P(rows, None, None), P(mlp), P(mlp, None, req), P(mlp, None, req),
            P(), P(), P(), P(), P(), P(), P(), P(None, req, mlp), P(mlp, req),
        ),
        out_specs=(P(rows, None), P(rows, None)),
        check_vma=False,
    )
```

profile of v0, /device:TPU:1, one launch (start us, length us, event | category | flops | bytes accessed | tf_op | source)
XLA Modules:
  0.0 154.6 jit_solution(8288581927981184124)
XLA Ops:
  1.3 0.8 pad_maximum_fusion.1
  2.0 0.1 copy.31
  2.2 0.9 copy.39
  3.1 0.1 pad.32.clone
  3.2 0.1 maximum_maximum_fusion
  3.4 0.1 pad.29.clone
  3.4 0.7 maximum_maximum_fusion.2.prefix_in
  4.2 0.9 fusion.2
  5.1 0.6 pad.23.slot_two_ref
  5.7 0.6 pad.24.slot_one_ref
  6.4 0.0 copy-start
  6.4 0.0 copy-start.8
  6.4 0.0 copy-start.2
  6.4 0.0 copy-start.1
  6.4 0.0 copy-start.3
  6.4 0.0 copy-start.7
  6.4 0.0 copy-start.4
  6.4 0.0 copy-start.5
  6.4 0.0 copy-start.6
  6.4 8.0 %copy.32.cache_in = f32[4,273,1792]{2,1,0:T(8,128)} copy(f32[4,273,1792]{2,0,1:T(4,128)} %param.26) | data formatting | bytes 15654912 | tf_op args[6]
  14.4 0.0 copy-done
  14.4 0.7 pad_maximum_fusion.gate_in
  15.2 0.0 copy-done.8
  15.2 0.1 broadcast_in_dim.39
  15.2 0.1 pad.39.clone
  15.3 0.0 copy-done.2
  15.3 0.7 maximum_maximum_fusion.1.keysum_ref
  16.1 0.0 copy-done.1
  16.1 0.7 pad.25.down_in
  16.7 0.6 slice_bitcast_fusion.1.up_in
  17.4 0.0 copy-done.3
  17.4 0.6 pad.22.slots_ref
  18.0 0.0 copy-done.7
  18.0 0.6 pad_convert_fusion.edge_ref
  18.6 0.0 copy-done.4
  18.6 0.6 broadcast_in_dim.41.conv_gain_ref
  19.2 0.0 copy-done.5
  19.2 0.6 broadcast_in_dim.42.attend_gain_ref
  19.9 0.0 copy-done.6
  19.9 0.6 broadcast_in_dim.43.hidden_gain_ref
  20.5 129.9 %shard_map.203 = bf16[272,1792]{1,0:T(8,128)(2,1)} custom-call(bf16[256,1792]{1,0:T(8,128)(2,1)} %rows_ref.1, f32[8,1792]{1,0:T(8,128)} %pad_convert_fusion.edge_ref, bf16[16,1792]{1,0:T(8,128)(2,1)} %pad.22.slots_ref, bf16[16,1792]{1,0:T(8,128)(2,1)} %pad.23.slot_two_ref, bf16[16,1792]{1,0:T(8,128)(2,1)} %pad.24.slot_one_ref, ...), custom_call_target="tpu_custom_call" | custom-call | tf_op jit(solution)/shard_map/pallas_call | solution.py:387
  150.4 2.2 %slice.39 = bf16[256,1792]{1,0:T(8,128)(2,1)} slice(bf16[272,1792]{1,0:T(8,128)(2,1)} %shard_map.203), slice={[0:256], [0:1792]} | slice | bytes 1835008 | tf_op jit(solution)/shard_map/slice | solution.py:430
  152.5 0.7 broadcast_compare_fusion
  153.2 1.4 slice_select_fusion
  (10 shorter events, 0.1 us)
Async XLA Ops:
  6.4 8.0 %copy-start = (bf16[2,112,448]{2,1,0:T(8,128)(2,1)S(1)}, bf16[2,112,448]{2,1,0:T(8,128)(2,1)}, u32[]{:S(2)}) copy-start(bf16[2,112,448]{2,1,0:T(8,128)(2,1)} %param.38) | copy-start | bytes 602116
  6.4 8.8 %copy-start.8 = (s32[4]{0:T(128)S(1)}, s32[4]{0:T(128)}, u32[]{:S(2)}) copy-start(s32[4]{0:T(128)} %param.25) | copy-start | bytes 52
  6.4 9.0 %copy-start.2 = (f32[4,272,16]{1,2,0:T(8,128)S(1)}, f32[4,272,16]{1,2,0:T(8,128)}, u32[]{:S(2)}) copy-start(f32[4,272,16]{1,2,0:T(8,128)} %param.27) | copy-start | bytes 208900
  6.4 9.7 %copy-start.1 = (bf16[448,112]{1,0:T(8,128)(2,1)S(1)}, bf16[448,112]{1,0:T(8,128)(2,1)}, u32[]{:S(2)}) copy-start(bf16[448,112]{1,0:T(8,128)(2,1)} %param.39) | copy-start | bytes 301060
  6.4 11.0 %copy-start.3 = (bf16[4,1792]{1,0:T(4,128)(2,1)S(1)}, bf16[4,1792]{1,0:T(4,128)(2,1)}, u32[]{:S(2)}) copy-start(bf16[4,1792]{1,0:T(4,128)(2,1)} %param.22) | copy-start | bytes 43012
  6.4 11.6 %copy-start.7 = (bf16[1,2,1792]{2,1,0:T(2,128)(2,1)S(1)}, bf16[1,2,1792]{2,1,0:T(2,128)(2,1)}, u32[]{:S(2)}) copy-start(bf16[1,2,1792]{2,1,0:T(2,128)(2,1)} %param.21) | copy-start | bytes 21508
  6.4 12.2 %copy-start.4 = (f32[1792]{0:T(1024)S(1)}, f32[1792]{0:T(1024)}, u32[]{:S(2)}) copy-start(f32[1792]{0:T(1024)} %param.31) | copy-start | bytes 21508
  6.4 12.8 %copy-start.5 = (f32[1792]{0:T(1024)S(1)}, f32[1792]{0:T(1024)}, u32[]{:S(2)}) copy-start(f32[1792]{0:T(1024)} %param.33) | copy-start | bytes 21508
  6.4 13.4 %copy-start.6 = (f32[1792]{0:T(1024)S(1)}, f32[1792]{0:T(1024)}, u32[]{:S(2)}) copy-start(f32[1792]{0:T(1024)} %param.37) | copy-start | bytes 21508
where the time goes:
time: 155 us
  Pallas kernels  130 us (84%)
  local copies, waits for them, and re-layouts  17.5 us (11%)
  other arithmetic  5.82 us (4%)
    pallas_call x1, Pallas kernels, on_device(): pl.pallas_call(layer_kernel, out_shape=jax.ShapeDtypeStruct((R, D), BF),...  130 us
    unnamed x20, local copies, waits for them, and re-layouts  8.93 us

commit v1 on v0

--- a/solution.py
+++ b/solution.py
@@ -40,12 +40,12 @@
 
 
 def layer_kernel(
-    rows_ref, edge_ref, slots_ref, slot_two_ref, slot_one_ref, keysum_ref,
-    conv_gain_ref, taps_ref, attend_gain_ref, hidden_gain_ref,
-    gate_in, down_in, up_in, prefix_in, cache_in, wf_in, wv_in, wo_in,
-    out_ref,
+    rows_ref, edge_ref, slots_ref, slot_edge_ref, keysum_ref, gains_ref, taps_ref,
+    prefix_state_ref, prefix_keys_ref, prefix_length_ref, length_ref, live_ref,
+    feed_in, down_in, cache_in, wf_in, wv_in, wo_in,
+    out_ref, slot_out_ref,
     gate, down, up, prefix, wf, wv, wo, cache,
-    big, conv, ain, qk, rep, slot_att, pair, tok, attended, hid, give, take, fin,
+    big, conv, ain, qk, rep, slot_att, pair, tok, attended, hid, give, take, fin, slot_rows,
     local_sem, cache_sem, send_sem, recv_sem, swap_send, swap_recv,
 ):
     my = {a: lax.axis_index(a) for a in ("z", "y", "x")}
@@ -62,7 +62,7 @@
         local.append(copy)
     cache_copies = []
     for n in range(4):
-        cache_copies.append(pltpu.make_async_copy(cache_in.at[n], cache.at[n % 2], cache_sem.at[n]))
+        cache_copies.append(pltpu.make_async_copy(cache_in.at[:, n], cache.at[n % 2], cache_sem.at[n]))
     cache_copies[0].start()
     cache_copies[1].start()
 
@@ -86,10 +86,23 @@
             pl.semaphore_signal(barrier, inc=1, device_id={axis: near(axis, step)}, device_id_type=MESH)
     pl.semaphore_signal(barrier, inc=1, device_id={"c": other}, device_id_type=MESH)
     own = []
-    for part, source in ((PREFIX, prefix_in), (GATE, gate_in), (DOWN, down_in), (UP, up_in)):
+    for part, source in (
+        (GATE, feed_in.at[:, pl.ds(0, 512)]), (DOWN, down_in), (UP, feed_in.at[:, pl.ds(512, 384)])):
         copy = pltpu.make_async_copy(source, view(part, my), local_sem.at[part])
         copy.start()
         own.append(copy)
+
+    key_column = jnp.sum(
+        jnp.where(iota((NF - 1, NF - 1), 0) == iota((NF - 1, NF - 1), 1), prefix_keys_ref[...], 0.0),
+        axis=1, keepdims=True)
+    own_prefix = prefix.at[my["z"], my["y"]]
+    square = jnp.where(iota((256, 128), 1) == DV, key_column[16:272], prefix_state_ref[17:273, :])
+    own_prefix[0:256, :] = (square * (2.0 * FD) ** (-0.5)).astype(BF)
+    linear = jnp.where(iota((16, 128), 1) == DV, key_column[0:16], prefix_state_ref[1:17, :])
+    own_prefix[256:272, :] = (linear * FD ** (-0.25)).astype(BF)
+    constant = jnp.where(
+        iota((16, 128), 1) == DV, prefix_length_ref[0].astype(F32), prefix_state_ref[0:1, :])
+    own_prefix[272:288, :] = jnp.where(iota((16, 128), 0) == 0, constant, 0.0).astype(BF)
     pl.semaphore_wait(barrier, 7)
     for copy in own:
         copy.wait()
@@ -166,8 +179,9 @@
     for part in everything:
         phase_one(part)
 
-    conv_gain = conv_gain_ref[...]
-    big[0:8, 0:D] = edge_ref[...]
+    conv_gain = gains_ref[0:1, :]
+    big[0:8, 0:D] = jnp.zeros((8, D), F32)
+    big[6:8, 0:D] = edge_ref[...].astype(F32)
 
     def norm_rows(i, _):
         at = pl.multiple_of(i * 16, 16)
@@ -182,7 +196,7 @@
     def gated(rows, u, one, two):
         convolved = taps_ref[0:1, :] * u + taps_ref[1:2, :] * one + taps_ref[2:3, :] * two
         mixed = (rows.astype(F32) + convolved * jax.nn.sigmoid(u)).astype(BF)
-        return mixed, norm(mixed.astype(F32), attend_gain_ref[...]).astype(BF)
+        return mixed, norm(mixed.astype(F32), gains_ref[1:2, :]).astype(BF)
 
     def conv_rows(i, _):
         at = pl.multiple_of(i * 16, 16)
@@ -194,8 +208,14 @@
         return 0
 
     lax.fori_loop(0, T // 16, conv_rows, 0)
-    slot_u = norm(slots_ref[...].astype(F32), conv_gain).astype(BF).astype(F32)
-    mixed, normed = gated(slots_ref[...], slot_u, slot_one_ref[...].astype(F32), slot_two_ref[...].astype(F32))
+    slot_rows[...] = jnp.zeros_like(slot_rows)
+    slot_rows[0, 0:4, :] = slots_ref[...].astype(F32)
+    for n in range(4):
+        before = slot_edge_ref[n].astype(F32)
+        slot_rows[2, n:n + 1, :] = before[0:1]
+        slot_rows[1, n:n + 1, :] = before[1:2]
+    slot_u = norm(slot_rows[0], conv_gain).astype(BF).astype(F32)
+    mixed, normed = gated(slot_rows[0], slot_u, slot_rows[1], slot_rows[2])
     conv[T:R, :] = mixed
     ain[T:R, :] = normed
 
@@ -244,7 +264,9 @@
         weight = 1.0 + s + 0.5 * s * s
         qb = q.astype(BF)
         phi = (dot(qb, first_sel) + first_add) * (dot(qb, second_sel) * (2.0 * FD) ** (-0.5) + second_add)
-        den = jnp.sum(phi * keysum_ref[n], axis=-1, keepdims=True) + weight
+        rest = jnp.where(column == 0, 0.0, phi)[:, 0:NF]
+        sums = pltpu.roll(keysum_ref[n], 1, 1)[:, 0:NF]
+        den = jnp.sum(rest * sums, axis=-1, keepdims=True) + length_ref[n].astype(F32) + weight
         phi_high = phi.astype(BF)
         num = dot(phi_high[:, 0:NF], cache[n % 2].astype(BF))
         if n + 2 < 4:
@@ -304,7 +326,7 @@
         at = pl.multiple_of(i * 16, 16)
         mixed = (conv[pl.ds(at, 16), :].astype(F32) + big[pl.ds(pl.multiple_of(R + at, 16), 16), 0:D]).astype(BF)
         attended[pl.ds(at, 16), :] = mixed
-        tok[core, pl.ds(at, 16), :] = norm(mixed.astype(F32), hidden_gain_ref[...]).astype(BF)
+        tok[core, pl.ds(at, 16), :] = norm(mixed.astype(F32), gains_ref[2:3, :]).astype(BF)
         return 0
 
     lax.fori_loop(0, R // 16, hidden_rows, 0)
@@ -359,7 +381,11 @@
         start = r * DV // 128 * 128
         piece = pltpu.roll(jnp.concatenate([piece, jnp.zeros_like(piece)], axis=1), r * DV - start, 1)
         fin[:, start:start + 256] += piece
-    out_ref[...] = fin[:, 0:D].astype(BF)
+    out_ref[...] = fin[0:T, 0:D].astype(BF)
+    live = iota((4, D), 0)
+    for n in range(4):
+        live = jnp.where(iota((4, D), 0) == n, live_ref[n], live)
+    slot_out_ref[...] = jnp.where(live == 1, fin[T:T + 4, 0:D], 0.0).astype(BF)
     for copy in started:
         copy.wait_send()
 
@@ -369,26 +395,19 @@
     cache_keysum, prefix_length, prefix_state, prefix_keysum, conv_gain, conv_taps, attend_gain,
     feature_weight, value_weight, output_weight, hidden_gain, gate_up, down_weight,
 ):
-    gate_in = jnp.concatenate([gate_up[0], gate_up[1, :, 384:]], axis=1)
-    up_in = gate_up[1, :, :384]
+    feed_in = jnp.concatenate([gate_up[0], gate_up[1, :, 384:], gate_up[1, :, :384]], axis=1)
     down_in = jnp.pad(down_weight, ((0, 0), (0, 16)))
-    sums = jnp.concatenate([prefix_length.astype(F32)[:, None], prefix_keysum[0]], axis=0)
-    state = jnp.concatenate([prefix_state[0], sums, jnp.zeros((NF, 15), F32)], axis=1)
-    prefix_in = jnp.concatenate([
-        state[17:] * (2.0 * FD) ** (-0.5), state[1:17] * FD ** (-0.25), state[0:1], jnp.zeros((15, 128), F32)],
-        axis=0).astype(BF)
-    lengths = jnp.broadcast_to(cache_length.astype(F32)[:, None, None], (4, H, 1))
-    keysum = jnp.concatenate(
-        [lengths, jnp.transpose(cache_keysum, (0, 2, 1)), jnp.zeros((4, H, 384 - NF), F32)], axis=2)
-    edge = jnp.pad(prompt_edge[0].astype(F32), ((6, 0), (0, 0)))
-    spare = ((0, 12), (0, 0))
+    state_in = jnp.pad(prefix_state[0], ((0, 15), (0, 16)))
+    keysum = jnp.pad(jnp.transpose(cache_keysum, (0, 2, 1)), ((0, 0), (0, 0), (0, 112)))
+    gains = jnp.stack([conv_gain, attend_gain, hidden_gain])
     vmem = pl.BlockSpec(memory_space=pltpu.VMEM)
+    smem = pl.BlockSpec(memory_space=pltpu.SMEM)
     hbm = pl.BlockSpec(memory_space=pl.ANY)
-    out = pl.pallas_call(
+    return pl.pallas_call(
         layer_kernel,
-        out_shape=jax.ShapeDtypeStruct((R, D), BF),
-        in_specs=[vmem] * 10 + [hbm] * 8,
-        out_specs=vmem,
+        out_shape=(jax.ShapeDtypeStruct((T, D), BF), jax.ShapeDtypeStruct((4, D), BF)),
+        in_specs=[vmem] * 9 + [smem] * 3 + [hbm] * 6,
+        out_specs=(vmem, vmem),
         scratch_shapes=[
             pltpu.VMEM((4, 4, 4, 112, 512), BF),
             pltpu.VMEM((4, 448, 2048), BF),
@@ -411,6 +430,7 @@
             pltpu.VMEM((R, 2048), BF),
             pltpu.VMEM((R, 2048), BF),
             pltpu.VMEM((R, D + 128), F32),
+            pltpu.VMEM((3, 16, D), F32),
             pltpu.SemaphoreType.DMA((7,)),
             pltpu.SemaphoreType.DMA((4,)),
             pltpu.SemaphoreType.DMA((4, 15)),
@@ -421,13 +441,11 @@
         compiler_params=pltpu.CompilerParams(
             collective_id=0, has_side_effects=True, vmem_limit_bytes=67043328),
     )(
-        prompt_rows, edge, jnp.pad(decode_rows, spare), jnp.pad(decode_edge[:, 0], spare),
-        jnp.pad(decode_edge[:, 1], spare), keysum, conv_gain[None], conv_taps, attend_gain[None],
-        hidden_gain[None], gate_in, down_in, up_in, prefix_in, cache_state, feature_weight,
-        value_weight, output_weight,
+        prompt_rows, prompt_edge[0], decode_rows, decode_edge, keysum, gains, conv_taps,
+        state_in, jnp.transpose(prefix_keysum[0]), prefix_length, cache_length, decode_live,
+        feed_in, down_in, jnp.transpose(cache_state, (1, 0, 2)), feature_weight, value_weight,
+        output_weight,
     )
-    slots = out[T:T + 4]
-    return out[:T], jnp.where(decode_live[:, None] == 1, slots, jnp.zeros_like(slots))
 
 
 def solution(mesh):

time: 155 us -> 146 us (0.942)
  local copies, waits for them, and re-layouts: 17.5 us -> 12.8 us
  other arithmetic: 5.82 us -> 1.39 us
    unnamed x20 -> x3, local copies, waits for them, and re-layouts: 8.93 us -> 4.4 us
    slice x3 -> x0, local copies, waits for them, and re-layouts: 3.04 us -> none  [the longest x1 2.16 us: on_device(): out[:T]]
    concatenate x5 -> x1, other arithmetic: 3.07 us -> 0.77 us  [on_device(): jnp.concatenate([gate_up[0], gate_up[1, :, 384:], gate_up[1, :, :384]], a...]
    another operation x0 -> x3, local copies, waits for them, and re-layouts: none -> 2.11 us  [on_device(): gains = jnp.stack([conv_gain, attend_gain, hidden_gain])]
    broadcast_in_dim x7 -> x0, local copies, waits for them, and re-layouts: 1.9 us -> none  [the longest x1 0.61 us: on_device(): attend_gain[None]]
    squeeze x4 -> x3, local copies, waits for them, and re-layouts: 0.67 us -> 2.55 us  [the longest x1 0.91 us: on_device(): gate_up[0]]
where the time goes in v1:
time: 146 us; the launch traced here: 145 us
  Pallas kernels  130 us (89%)
  local copies, waits for them, and re-layouts  12.8 us (9%)
    pallas_call x1, Pallas kernels, on_device(): pl.pallas_call(layer_kernel, out_shape=(jax.ShapeDtypeStruct((T, D), BF),...  130 us
    unnamed x3, local copies, waits for them, and re-layouts  4.4 us

profile of v1, /device:TPU:1, one launch (start us, length us, event | category | flops | bytes accessed | tf_op | source)
XLA Modules:
  0.0 145.3 jit_solution(14980460928989349711)
XLA Ops:
  1.3 0.7 stack.12
  2.0 0.7 stack.13
  2.7 0.7 stack.14
  3.4 0.6 pad_maximum_fusion.1.gains_ref
  4.0 0.8 slice_bitcast_fusion.2
  4.8 0.9 slice_bitcast_fusion.1
  5.7 1.5 %pad.12.keysum_ref = f32[4,16,384]{2,1,0:T(8,128)} pad(f32[4,16,272]{2,1,0:T(8,128)} %bitcast.15, f32[]{:T(128)} %constant.3.clone.1), padding=0_0x0_0x0_112 | pad | bytes 167940 | tf_op jit(solution)/shard_map/jit(_pad)/pad | solution.py:401
  7.2 1.6 %pad.14.down_in = bf16[448,128]{1,0:T(8,128)(2,1)} pad(bf16[448,112]{1,0:T(8,128)(2,1)} %param.39, bf16[]{:T(256)} %constant.4.clone.1), padding=0_0x0_16 | pad | bytes 215042 | tf_op jit(solution)/shard_map/jit(_pad)/pad | solution.py:399
  8.8 0.9 slice_bitcast_fusion
  9.7 0.8 pad_maximum_fusion.feed_in
  10.4 0.9 copy.24
  11.4 0.7 pad.13.prefix_state_ref
  12.0 129.8 %shard_map.203 = (bf16[256,1792]{1,0:T(8,128)(2,1)}, bf16[4,1792]{1,0:T(4,128)(2,1)}) custom-call(bf16[256,1792]{1,0:T(8,128)(2,1)} %rows_ref.1, bf16[2,1792]{1,0:T(2,128)(2,1)} %bitcast.16, bf16[4,1792]{1,0:T(4,128)(2,1)} %slots_ref.1, bf16[4,2,1792]{2,1,0:T(2,128)(2,1)} %slot_edge_ref.1, f32[4,16,384]{2,1,0:T(8,128)} %pad.12.keysum_ref, ...), custom_call_target="tpu_custom_call" | custom-call | tf_op jit(solution)/shard_map/pallas_call | solution.py:406
  141.9 2.2 %copy.28 = bf16[256,1792]{1,0:T(8,128)(2,1)} copy(bf16[256,1792]{1,0:T(8,128)(2,1)} %get-tuple-element.4) | data formatting | bytes 1835008
  144.0 1.3 copy.29

commit v2 on v1

--- a/solution.py
+++ b/solution.py
@@ -42,10 +42,10 @@
 def layer_kernel(
     rows_ref, edge_ref, slots_ref, slot_edge_ref, keysum_ref, gains_ref, taps_ref,
     prefix_state_ref, prefix_keys_ref, prefix_length_ref, length_ref, live_ref,
-    feed_in, down_in, cache_in, wf_in, wv_in, wo_in,
+    gate_up_ref, down_ref, cache_in, wf_in, wv_in, wo_in,
     out_ref, slot_out_ref,
     gate, down, up, prefix, wf, wv, wo, cache,
-    big, conv, ain, qk, rep, slot_att, pair, tok, attended, hid, give, take, fin, slot_rows,
+    big, conv, ain, qk, rep, slot_att, pair, tok, attended, hid, give, take, fin, slot_rows, stage, sums_row,
     local_sem, cache_sem, send_sem, recv_sem, swap_send, swap_recv,
 ):
     my = {a: lax.axis_index(a) for a in ("z", "y", "x")}
@@ -57,7 +57,7 @@
 
     local = []
     for k, (source, target) in enumerate(((wf_in, wf), (wv_in, wv), (wo_in, wo.at[pl.ds(0, D)]))):
-        copy = pltpu.make_async_copy(source, target, local_sem.at[4 + k])
+        copy = pltpu.make_async_copy(source, target, local_sem.at[k])
         copy.start()
         local.append(copy)
     cache_copies = []
@@ -85,13 +85,16 @@
         for step in (1, -1):
             pl.semaphore_signal(barrier, inc=1, device_id={axis: near(axis, step)}, device_id_type=MESH)
     pl.semaphore_signal(barrier, inc=1, device_id={"c": other}, device_id_type=MESH)
-    own = []
-    for part, source in (
-        (GATE, feed_in.at[:, pl.ds(0, 512)]), (DOWN, down_in), (UP, feed_in.at[:, pl.ds(512, 384)])):
-        copy = pltpu.make_async_copy(source, view(part, my), local_sem.at[part])
-        copy.start()
-        own.append(copy)
-
+    own_gate = gate.at[my["x"], my["z"], my["y"]]
+    own_gate[:, 0:384] = gate_up_ref[0, :, 0:384]
+    stage[0:112, 0:64] = gate_up_ref[0, :, 384:448].astype(F32)
+    stage[112:224, 0:64] = gate_up_ref[1, :, 384:448].astype(F32)
+    tail = jnp.where(iota((112, 128), 1) < 64, stage[0:112, :], pltpu.roll(stage[112:224, :], 64, 1))
+    own_gate[:, 384:512] = tail.astype(BF)
+    up[my["x"], my["z"], my["y"]] = gate_up_ref[1, :, 0:384]
+    stage[:, 0:DV] = down_ref[...].astype(F32)
+    own_lanes = pl.ds(pl.multiple_of(my["y"] * 512 + my["z"] * 128, 128), 128)
+    down[my["x"], :, own_lanes] = jnp.where(iota((448, 128), 1) < DV, stage[...], 0.0).astype(BF)
     key_column = jnp.sum(
         jnp.where(iota((NF - 1, NF - 1), 0) == iota((NF - 1, NF - 1), 1), prefix_keys_ref[...], 0.0),
         axis=1, keepdims=True)
@@ -104,8 +107,6 @@
         iota((16, 128), 1) == DV, prefix_length_ref[0].astype(F32), prefix_state_ref[0:1, :])
     own_prefix[272:288, :] = jnp.where(iota((16, 128), 0) == 0, constant, 0.0).astype(BF)
     pl.semaphore_wait(barrier, 7)
-    for copy in own:
-        copy.wait()
 
     started = []
 
@@ -257,6 +258,7 @@
     slot_qk = qk[T:R, :].astype(F32)
     slot_v = big[T:R, 0:D]
     slot_att[...] = jnp.zeros_like(slot_att)
+    sums_row[...] = jnp.zeros_like(sums_row)
     for n in range(4):
         cache_copies[n].wait()
         q = jnp.where(head_of, slot_qk[n:n + 1, 0:256], 0.0)
@@ -265,7 +267,8 @@
         qb = q.astype(BF)
         phi = (dot(qb, first_sel) + first_add) * (dot(qb, second_sel) * (2.0 * FD) ** (-0.5) + second_add)
         rest = jnp.where(column == 0, 0.0, phi)[:, 0:NF]
-        sums = pltpu.roll(keysum_ref[n], 1, 1)[:, 0:NF]
+        sums_row[:, 0:NF - 1] = keysum_ref[n]
+        sums = pltpu.roll(sums_row[...], 1, 1)[:, 0:NF]
         den = jnp.sum(rest * sums, axis=-1, keepdims=True) + length_ref[n].astype(F32) + weight
         phi_high = phi.astype(BF)
         num = dot(phi_high[:, 0:NF], cache[n % 2].astype(BF))
@@ -395,10 +398,8 @@
     cache_keysum, prefix_length, prefix_state, prefix_keysum, conv_gain, conv_taps, attend_gain,
     feature_weight, value_weight, output_weight, hidden_gain, gate_up, down_weight,
 ):
-    feed_in = jnp.concatenate([gate_up[0], gate_up[1, :, 384:], gate_up[1, :, :384]], axis=1)
-    down_in = jnp.pad(down_weight, ((0, 0), (0, 16)))
     state_in = jnp.pad(prefix_state[0], ((0, 15), (0, 16)))
-    keysum = jnp.pad(jnp.transpose(cache_keysum, (0, 2, 1)), ((0, 0), (0, 0), (0, 112)))
+    keysum = jnp.transpose(cache_keysum, (0, 2, 1))
     gains = jnp.stack([conv_gain, attend_gain, hidden_gain])
     vmem = pl.BlockSpec(memory_space=pltpu.VMEM)
     smem = pl.BlockSpec(memory_space=pltpu.SMEM)
@@ -406,7 +407,7 @@
     return pl.pallas_call(
         layer_kernel,
         out_shape=(jax.ShapeDtypeStruct((T, D), BF), jax.ShapeDtypeStruct((4, D), BF)),
-        in_specs=[vmem] * 9 + [smem] * 3 + [hbm] * 6,
+        in_specs=[vmem] * 9 + [smem] * 3 + [vmem] * 2 + [hbm] * 4,
         out_specs=(vmem, vmem),
         scratch_shapes=[
             pltpu.VMEM((4, 4, 4, 112, 512), BF),
@@ -431,7 +432,9 @@
             pltpu.VMEM((R, 2048), BF),
             pltpu.VMEM((R, D + 128), F32),
             pltpu.VMEM((3, 16, D), F32),
-            pltpu.SemaphoreType.DMA((7,)),
+            pltpu.VMEM((448, 128), F32),
+            pltpu.VMEM((16, 384), F32),
+            pltpu.SemaphoreType.DMA((3,)),
             pltpu.SemaphoreType.DMA((4,)),
             pltpu.SemaphoreType.DMA((4, 15)),
             pltpu.SemaphoreType.DMA((4, 15)),
@@ -443,7 +446,7 @@
     )(
         prompt_rows, prompt_edge[0], decode_rows, decode_edge, keysum, gains, conv_taps,
         state_in, jnp.transpose(prefix_keysum[0]), prefix_length, cache_length, decode_live,
-        feed_in, down_in, jnp.transpose(cache_state, (1, 0, 2)), feature_weight, value_weight,
+        gate_up, down_weight, jnp.transpose(cache_state, (1, 0, 2)), feature_weight, value_weight,
         output_weight,
     )
 

time: 146 us -> 134 us (0.918)
  Pallas kernels: 130 us -> 124 us
  local copies, waits for them, and re-layouts: 12.8 us -> 7.18 us
    pallas_call x1, Pallas kernels: 130 us -> 124 us  [on_device(): pl.pallas_call(layer_kernel, out_shape=(jax.ShapeDtypeStruct((T, D), BF),...]
    pad x2 -> x0, local copies, waits for them, and re-layouts: 3.11 us -> none  [the longest x1 1.57 us: on_device(): down_in = jnp.pad(down_weight, ((0, 0), (0, 16)))]
    squeeze x3 -> x0, local copies, waits for them, and re-layouts: 2.55 us -> none  [the longest x1 0.91 us: on_device(): gate_up[0]]
where the time goes in v2:
time: 134 us
  Pallas kernels  124 us (93%)
  local copies, waits for them, and re-layouts  7.18 us (5%)
    pallas_call x1, Pallas kernels, on_device(): pl.pallas_call(layer_kernel, out_shape=(jax.ShapeDtypeStruct((T, D), BF),...  124 us
    unnamed x3, local copies, waits for them, and re-layouts  4.4 us

profile of v2, /device:TPU:1, one launch (start us, length us, event | category | flops | bytes accessed | tf_op | source)
XLA Modules:
  0.0 133.6 jit_solution(16460770145293792700)
XLA Ops:
  1.3 0.7 stack.12
  2.0 0.7 stack.13
  2.7 0.7 stack.14
  3.4 0.6 pad_maximum_fusion.gains_ref
  4.0 0.9 copy.24
  4.9 0.7 pad.4.prefix_state_ref
  5.6 124.5 %shard_map.203 = (bf16[256,1792]{1,0:T(8,128)(2,1)}, bf16[4,1792]{1,0:T(4,128)(2,1)}) custom-call(bf16[256,1792]{1,0:T(8,128)(2,1)} %rows_ref.1, bf16[2,1792]{1,0:T(2,128)(2,1)} %bitcast.10, bf16[4,1792]{1,0:T(4,128)(2,1)} %slots_ref.1, bf16[4,2,1792]{2,1,0:T(2,128)(2,1)} %slot_edge_ref.1, f32[4,16,272]{2,1,0:T(8,128)} %bitcast.9, ...), custom_call_target="tpu_custom_call" | custom-call | tf_op jit(solution)/shard_map/pallas_call | solution.py:407
  130.1 2.2 %copy.28 = bf16[256,1792]{1,0:T(8,128)(2,1)} copy(bf16[256,1792]{1,0:T(8,128)(2,1)} %get-tuple-element.4) | data formatting | bytes 1835008
  132.3 1.3 copy.29
